TPU v7x, 128 devices: a whole 4x4x4 slice. The times are simulated.
128 devices in a mesh: tile: 64 (over z, x_lo, y, core), mem: 2 (over x_hi).
Axes of the slice: x: 4 (x_hi: 2, x_lo: 2; x = x_hi * 2 + x_lo), y: 4, z: 4, core: 2. Of those that a mesh axis runs over, the one named last changes fastest.
Arguments:
- control: bfloat16 [4, 64, 768, 1536], P('mem', None, 'tile'), may hold values from -6 to 6
- members: bfloat16 [4, 64, 768, 1536], P('mem', None, 'tile'), may hold values from -6 to 6
- gradient: bfloat16 [64, 768, 1536], P('tile'), may hold values from -6 to 6
- step_x: float32 [1536], replicated, may hold values from 0.1 to 0.4
- step_y: float32 [768], replicated, may hold values from 0.01 to 0.1
- step_z: float32 [64], replicated, may hold values from 0.1 to 1
Outputs:
- increment: bfloat16 [64, 768, 1536], P('tile')
- control_grad: bfloat16 [4, 64, 768, 1536], P('mem', None, 'tile')
All inputs are finite; a program needn't handle non-finite values.
Results may differ from a plain program's by a relative error of at most 0.0085.
Values may be sent and summed in bfloat16 or wider, within the bound.
A program may use at most 128 MiB of HBM per device.

v0:
```python
import jax
import jax.numpy as jnp
from jax import lax
from jax.sharding import PartitionSpec as P

BAND = 8
along_gain = 0.35
horiz_gain = 0.15
vert_gain = 0.5


def kernel_matrix(steps, gain):
    coord = jnp.cumsum(steps)
    return gain * jnp.exp(-jnp.abs(coord[:, None] - coord[None, :]))


def build_filters(step_x, step_y, step_z):
    filter_x = kernel_matrix(step_x, along_gain).astype(jnp.bfloat16)
    filter_y = kernel_matrix(step_y, horiz_gain).astype(jnp.bfloat16)
    level_ids = jnp.arange(step_z.shape[0], dtype=jnp.int32)
    banded = jnp.abs(level_ids[:, None] - level_ids[None, :]) <= BAND
    filter_z = jnp.where(banded, kernel_matrix(step_z, vert_gain), jnp.float32(0.0)).astype(
        jnp.bfloat16
    )
    return (filter_x, filter_y, filter_z)


def body(control, members, gradient, step_x, step_y, step_z):
    filter_x, filter_y, filter_z = build_filters(step_x, step_y, step_z)

    def filter_along_x(fields):
        return jnp.einsum(
            "mzyk,kx->mzyx", fields, filter_x, preferred_element_type=jnp.float32
        ).astype(jnp.bfloat16)

    def filter_along_y(fields):
        return jnp.einsum(
            "yk,mzkx->mzyx", filter_y, fields, preferred_element_type=jnp.float32
        ).astype(jnp.bfloat16)

    vert = jnp.einsum(
        "zw,mwyx->mzyx", filter_z, control, preferred_element_type=jnp.float32
    ).astype(jnp.bfloat16)
    along = filter_along_x(vert)
    grad_rows = lax.all_to_all(gradient, "tile", split_axis=1, concat_axis=0, tiled=True)
    weighted = (members.astype(jnp.float32) * grad_rows.astype(jnp.float32)[None]).astype(
        jnp.bfloat16
    )
    level_along, level_weighted = (
        lax.all_to_all(along, "tile", split_axis=1, concat_axis=2, tiled=True),
        lax.all_to_all(weighted, "tile", split_axis=1, concat_axis=2, tiled=True),
    )
    shaped = filter_along_y(level_along)
    adj_x = filter_along_x(filter_along_y(level_weighted))
    row_shaped, row_adjoint = (
        lax.all_to_all(shaped, "tile", split_axis=2, concat_axis=1, tiled=True),
        lax.all_to_all(adj_x, "tile", split_axis=2, concat_axis=1, tiled=True),
    )
    partial_sum = jnp.sum(members.astype(jnp.float32) * row_shaped.astype(jnp.float32), axis=0)
    group_total = lax.psum(partial_sum, "mem")
    increment = lax.all_to_all(
        group_total.astype(jnp.bfloat16), "tile", split_axis=0, concat_axis=1, tiled=True
    )
    control_grad = jnp.einsum(
        "wz,mwyx->mzyx", filter_z, row_adjoint, preferred_element_type=jnp.float32
    ).astype(jnp.bfloat16)
    return (increment, control_grad)


def solution(mesh):
    placed = (
        P("mem", None, "tile", None),
        P("mem", None, "tile", None),
        P("tile", None, None),
        P(),
        P(),
        P(),
    )
    return jax.shard_map(
        body,
        mesh=mesh,
        in_specs=placed,
        out_specs=(P("tile", None, None), P("mem", None, "tile", None)),
        check_vma=False,
    )
```

profile of v0, /device:TPU:1, one launch (start us, length us, event | category | flops | bytes accessed | tf_op | source)
XLA Modules:
  0.0 557.3 jit_solution(10681981986497061035)
XLA Ops:
  0.6 1.0 reduce-window.31
  1.6 0.1 slice.18
  1.7 0.1 slice_reduce_fusion
  1.8 0.1 add_bitcast_fusion
  1.9 0.8 copy.36
  2.7 0.1 reduce-window.30
  2.8 0.1 reduce
  2.9 13.6 %fusion.16 = bf16[2,64,12,1536]{3,1,2,0:T(8,128)(2,1)} fusion(f32[1536]{0:T(1024)S(1)} %add_bitcast_fusion, bf16[2,64,12,1536]{3,1,2,0:T(8,128)(2,1)} %param.6, f32[64]{0:T(128)S(1)} %reduce), kind=kOutput, calls=%fused_computation.23 | convolution fusion | flops 7566299136 | bytes 9443584 | tf_op jit(solution)/shard_map/mzyk,kx->mzyx/dot_general | solution.py:32
  16.5 9.6 %copy.38 = bf16[2,64,12,1536]{3,0,2,1:T(2,128)(2,1)} copy(bf16[2,64,12,1536]{3,1,2,0:T(8,128)(2,1)} %fusion.16) | data formatting | bytes 9437184 | tf_op jit(solution)/shard_map/convert_element_type | solution.py:34
  26.0 0.0 copy-start
  26.0 11.2 %all-to-all-start = ((bf16[2,64,12,1536]{3,0,2,1:T(2,128)(2,1)}), bf16[2,64,12,1536]{3,0,2,1:T(2,128)(2,1)}, u32[]{:S(2)}, u32[]{:S(2)}) async-start(bf16[2,64,12,1536]{3,0,2,1:T(2,128)(2,1)} %copy.38), calls=%async_computation | async-start | bytes 9437184 | tf_op jit(solution)/shard_map/all_to_all | solution.py:50
  37.2 0.0 copy-done
  37.3 5.8 %copy.69 = bf16[1,768,1536]{2,0,1:T(2,128)(2,1)} copy(bf16[1,768,1536]{2,1,0:T(8,128)(2,1)S(1)} %copy-done) | data formatting | bytes 4718592 | tf_op args[2]
  43.1 0.5 broadcast.22
  43.6 15.7 %reduce.7 = bf16[768,1536]{1,0:T(8,128)(2,1)S(1)} reduce(bf16[768,1,1536]{2,1,0:T(2,128)(2,1)} %bitcast.65, bf16[]{:T(256)} %broadcast.22), dimensions={1}, to_apply=%bitcast.64.reduce_sub_computation | reduce | bytes 4718594
  59.3 0.0 copy-start.1
  59.3 2.5 reshape.162
  61.7 36.2 %all-to-all-done = bf16[2,64,12,1536]{3,0,2,1:T(2,128)(2,1)} async-done(((bf16[2,64,12,1536]{3,0,2,1:T(2,128)(2,1)}), bf16[2,64,12,1536]{3,0,2,1:T(2,128)(2,1)}, u32[]{:S(2)}, u32[]{:S(2)}) %all-to-all-start) | async-done | bytes 4718624 | tf_op jit(solution)/shard_map/all_to_all | solution.py:50
  97.9 4.4 all-to-all-start.3
  102.3 0.0 copy-done.1
  102.3 0.3 reduce-window.33
  102.6 0.1 slice.16
  102.7 0.1 slice_reduce_fusion.1
  102.8 0.1 add_bitcast_fusion.1
  102.9 8.4 %convert_bitcast_fusion.2 = bf16[2,1,768,1536]{2,3,0,1:T(8,128)(2,1)} fusion(bf16[2,768,1536]{2,0,1:T(2,128)(2,1)} %bitcast.7, f32[768]{0:T(1024)S(1)} %add_bitcast_fusion.1), kind=kOutput, calls=%fused_computation.21 | convolution fusion | flops 3629187072 | bytes 9440256 | tf_op jit(solution)/shard_map/yk,mzkx->mzyx/dot_general | solution.py:37
  111.3 12.7 %copy.40 = bf16[2,1,768,1536]{3,0,1,2:T(2,128)(2,1)} copy(bf16[2,1,768,1536]{2,3,0,1:T(8,128)(2,1)} %convert_bitcast_fusion.2) | data formatting | bytes 9437184 | tf_op jit(solution)/shard_map/convert_element_type | solution.py:39
  124.0 10.1 %all-to-all-done.3 = bf16[64,2,9216]{2,1,0:T(2,128)(2,1)S(1)} async-done(((bf16[64,2,9216]{2,1,0:T(2,128)(2,1)}), bf16[64,2,9216]{2,1,0:T(2,128)(2,1)S(1)}, u32[]{:S(2)}, u32[]{:S(2)}) %all-to-all-start.3) | async-done | bytes 2359328 | tf_op jit(solution)/shard_map/all_to_all | solution.py:45
  134.1 5.7 %all-to-all-start.1 = ((bf16[2,1,768,1536]{3,0,1,2:T(2,128)(2,1)}), bf16[2,1,768,1536]{3,0,1,2:T(2,128)(2,1)}, u32[]{:S(2)}, u32[]{:S(2)}) async-start(bf16[2,1,768,1536]{3,0,1,2:T(2,128)(2,1)} %copy.40), calls=%async_computation.1 | async-start | bytes 9437184 | tf_op jit(solution)/shard_map/all_to_all | solution.py:56
  139.7 6.7 %reshape.163 = bf16[768,1,1536]{2,1,0:T(2,128)(2,1)} reshape(bf16[64,2,9216]{2,1,0:T(2,128)(2,1)S(1)} %all-to-all-done.3) | data formatting | bytes 4718592
  146.4 16.9 %convert_reduce_fusion = f32[768,1536]{1,0:T(8,128)} fusion(bf16[768,1,1536]{2,1,0:T(2,128)(2,1)} %reshape.163), kind=kLoop, calls=%fused_computation.17 | loop fusion | flops 1179648 | bytes 7077888 | tf_op jit(solution)/shard_map/convert_element_type | solution.py:46
  163.4 6.1 %reshape.152 = f32[64,12,1536]{2,1,0:T(8,128)} reshape(f32[768,1536]{1,0:T(8,128)} %convert_reduce_fusion) | data formatting | bytes 9437184 | tf_op jit(solution)/shard_map/convert_element_type | solution.py:46
  169.5 30.9 %all-to-all-done.1 = bf16[2,1,768,1536]{3,0,1,2:T(2,128)(2,1)} async-done(((bf16[2,1,768,1536]{3,0,1,2:T(2,128)(2,1)}), bf16[2,1,768,1536]{3,0,1,2:T(2,128)(2,1)}, u32[]{:S(2)}, u32[]{:S(2)}) %all-to-all-start.1) | async-done | bytes 4718624 | tf_op jit(solution)/shard_map/all_to_all | solution.py:56
  200.3 28.4 %fusion.1 = (bf16[2,64,12,1536]{3,0,2,1:T(2,128)(2,1)}, f32[64,12,1536]{2,1,0:T(8,128)}) fusion(f32[64,12,1536]{2,1,0:T(8,128)} %reshape.152, bf16[2,64,12,1536]{3,1,2,0:T(8,128)(2,1)} %param.7, bf16[2,64,12,1536]{3,0,2,1:T(2,128)(2,1)} %bitcast.26), kind=kLoop, calls=%fused_computation.3 | loop fusion | flops 12976128 | bytes 23592960 | tf_op jit(solution)/shard_map/convert_element_type | solution.py:46
  228.8 5.3 all-to-all-start.4
  234.0 197.0 %all-reduce.1 = bf16[64,12,1536]{2,1,0:T(8,128)(2,1)} all-reduce(f32[64,12,1536]{2,1,0:T(8,128)} %get-tuple-element.3), channel_id=1, replica_groups=mesh['tile'=64,'mem'=2] {'mem'}, use_global_device_ids=true, to_apply=%region_6.7 | all-reduce | flops 1179648 | bytes 7077888 | tf_op jit(solution)/shard_map/psum | solution.py:60
  431.1 0.0 all-to-all-done.4
  431.1 10.3 %all-to-all-start.2 = ((bf16[64,12,1536]{2,1,0:T(8,128)(2,1)}), bf16[64,12,1536]{2,1,0:T(8,128)(2,1)S(1)}, u32[]{:S(2)}, u32[]{:S(2)}) async-start(bf16[64,12,1536]{2,1,0:T(8,128)(2,1)} %all-reduce.1), calls=%async_computation.2 | async-start | bytes 6291456 | tf_op jit(solution)/shard_map/all_to_all | solution.py:61
  441.3 23.2 %convert_bitcast_fusion.1 = bf16[2,1,768,1536]{3,2,0,1:T(8,128)(2,1)} fusion(f32[1536]{0:T(1024)S(1)} %add_bitcast_fusion, bf16[2,768,1536]{2,0,1:T(2,128)(2,1)} %bitcast.14, f32[768]{0:T(1024)S(1)} %add_bitcast_fusion.1), kind=kOutput, calls=%fused_computation.19 | convolution fusion | flops 10891100160 | bytes 9446400 | tf_op jit(solution)/shard_map/mzyk,kx->mzyx/dot_general | solution.py:32
  464.5 9.3 %copy.44 = bf16[2,1,768,1536]{3,0,1,2:T(2,128)(2,1)} copy(bf16[2,1,768,1536]{3,2,0,1:T(8,128)(2,1)} %convert_bitcast_fusion.1) | data formatting | bytes 9437184 | tf_op jit(solution)/shard_map/convert_element_type | solution.py:34
  473.9 9.1 %all-to-all-done.2 = bf16[64,12,1536]{2,1,0:T(8,128)(2,1)S(1)} async-done(((bf16[64,12,1536]{2,1,0:T(8,128)(2,1)}), bf16[64,12,1536]{2,1,0:T(8,128)(2,1)S(1)}, u32[]{:S(2)}, u32[]{:S(2)}) %all-to-all-start.2) | async-done | bytes 2359328 | tf_op jit(solution)/shard_map/all_to_all | solution.py:61
  483.0 5.7 %all-to-all-start.5 = ((bf16[2,1,768,1536]{3,0,1,2:T(2,128)(2,1)}), bf16[2,1,768,1536]{3,0,1,2:T(2,128)(2,1)}, u32[]{:S(2)}, u32[]{:S(2)}) async-start(bf16[2,1,768,1536]{3,0,1,2:T(2,128)(2,1)} %copy.44), calls=%async_computation.5 | async-start | bytes 9437184 | tf_op jit(solution)/shard_map/all_to_all | solution.py:57
  488.7 2.1 all_to_all.19
  490.8 57.8 %all-to-all-done.5 = bf16[2,1,768,1536]{3,0,1,2:T(2,128)(2,1)} async-done(((bf16[2,1,768,1536]{3,0,1,2:T(2,128)(2,1)}), bf16[2,1,768,1536]{3,0,1,2:T(2,128)(2,1)}, u32[]{:S(2)}, u32[]{:S(2)}) %all-to-all-start.5) | async-done | bytes 4718624 | tf_op jit(solution)/shard_map/all_to_all | solution.py:57
  548.6 8.3 %convert_bitcast_fusion = bf16[2,64,12,1536]{3,1,2,0:T(8,128)(2,1)} fusion(bf16[2,64,12,1536]{3,0,2,1:T(2,128)(2,1)} %bitcast.20, f32[64]{0:T(128)S(1)} %reduce), kind=kOutput, calls=%fused_computation.18 | convolution fusion | flops 304386048 | bytes 9437440 | tf_op jit(solution)/shard_map/wz,mwyx->mzyx/dot_general | solution.py:64
  (2 shorter events, 0.1 us)
Async XLA Ops:
  26.0 11.2 %copy-start = (bf16[1,768,1536]{2,1,0:T(8,128)(2,1)S(1)}, bf16[1,768,1536]{2,1,0:T(8,128)(2,1)}, u32[]{:S(2)}) copy-start(bf16[1,768,1536]{2,1,0:T(8,128)(2,1)} %param.8) | copy-start | bytes 7077892
  26.0 71.9 %all-to-all-start = ((bf16[2,64,12,1536]{3,0,2,1:T(2,128)(2,1)}), bf16[2,64,12,1536]{3,0,2,1:T(2,128)(2,1)}, u32[]{:S(2)}, u32[]{:S(2)}) async-start(bf16[2,64,12,1536]{3,0,2,1:T(2,128)(2,1)} %copy.38), calls=%async_computation | async-start | bytes 9437184 | tf_op jit(solution)/shard_map/all_to_all | solution.py:50
  59.3 43.1 %copy-start.1 = (f32[768]{0:T(1024)S(1)}, f32[768]{0:T(1024)}, u32[]{:S(2)}) copy-start(f32[768]{0:T(1024)} %param.10) | copy-start | bytes 9220
  97.9 36.1 %all-to-all-start.3 = ((bf16[64,2,9216]{2,1,0:T(2,128)(2,1)}), bf16[64,2,9216]{2,1,0:T(2,128)(2,1)S(1)}, u32[]{:S(2)}, u32[]{:S(2)}) async-start(bf16[64,2,9216]{2,1,0:T(2,128)(2,1)} %reshape.162), calls=%async_computation.3 | async-start | bytes 4718592 | tf_op jit(solution)/shard_map/all_to_all | solution.py:45
  134.1 66.3 %all-to-all-start.1 = ((bf16[2,1,768,1536]{3,0,1,2:T(2,128)(2,1)}), bf16[2,1,768,1536]{3,0,1,2:T(2,128)(2,1)}, u32[]{:S(2)}, u32[]{:S(2)}) async-start(bf16[2,1,768,1536]{3,0,1,2:T(2,128)(2,1)} %copy.40), calls=%async_computation.1 | async-start | bytes 9437184 | tf_op jit(solution)/shard_map/all_to_all | solution.py:56
  228.8 202.3 %all-to-all-start.4 = ((bf16[2,64,12,1536]{3,0,2,1:T(2,128)(2,1)}), bf16[2,64,12,1536]{3,0,2,1:T(2,128)(2,1)}, u32[]{:S(2)}, u32[]{:S(2)}) async-start(bf16[2,64,12,1536]{3,0,2,1:T(2,128)(2,1)} %get-tuple-element.2), calls=%async_computation.4 | async-start | bytes 9437184 | tf_op jit(solution)/shard_map/all_to_all | solution.py:51
  431.1 51.9 %all-to-all-start.2 = ((bf16[64,12,1536]{2,1,0:T(8,128)(2,1)}), bf16[64,12,1536]{2,1,0:T(8,128)(2,1)S(1)}, u32[]{:S(2)}, u32[]{:S(2)}) async-start(bf16[64,12,1536]{2,1,0:T(8,128)(2,1)} %all-reduce.1), calls=%async_computation.2 | async-start | bytes 6291456 | tf_op jit(solution)/shard_map/all_to_all | solution.py:61
  483.0 65.6 %all-to-all-start.5 = ((bf16[2,1,768,1536]{3,0,1,2:T(2,128)(2,1)}), bf16[2,1,768,1536]{3,0,1,2:T(2,128)(2,1)}, u32[]{:S(2)}, u32[]{:S(2)}) async-start(bf16[2,1,768,1536]{3,0,1,2:T(2,128)(2,1)} %copy.44), calls=%async_computation.5 | async-start | bytes 9437184 | tf_op jit(solution)/shard_map/all_to_all | solution.py:57
where the time goes:
time: 567 us; the launch traced here: 557 us
  blocking collectives  197 us (35%)
  waiting for transfers between devices  144 us (25%)
  other arithmetic  62.7 us (11%)
  local copies, waits for them, and re-layouts  56.4 us (10%)
  matrix products  53.5 us (9%)
  starting transfers between devices  42.5 us (7%)
    psum x1, blocking collectives, body(): group_total = lax.psum(partial_sum, 'mem')  197 us
    all_to_all x1, waiting for transfers between devices, body(): lax.all_to_all(adj_x, 'tile', split_axis=2, concat_axis=1, tiled=True)  57.8 us
    dot_general x2, matrix products, filter_along_x(): jnp.einsum('mzyk,kx->mzyx', fields, filter_x, preferred_element_type=jnp....  36.8 us
    all_to_all x1, waiting for transfers between devices, body(): lax.all_to_all(along, 'tile', split_axis=1, concat_axis=2, tiled=True)  36.2 us
    all_to_all x1, waiting for transfers between devices, body(): lax.all_to_all(shaped, 'tile', split_axis=2, concat_axis=1, tiled=True)  30.9 us
    convert_element_type x1, other arithmetic, body(): (members.astype(jnp.float32) * grad_rows.astype(jnp.float32)[None]).astyp...  28.4 us
    convert_element_type x2, local copies, waits for them, and re-layouts, filter_along_x(): return jnp.einsum('mzyk,kx->mzyx', fields, filter_x, preferred_element_ty...  18.9 us
    convert_element_type x1, other arithmetic, body(): grad_rows.astype(jnp.float32)[None]  16.9 us
  transfers between devices with their start and end apart: 6, of which 5 were waited for; matrix products, arithmetic and copies ran while one was open for 19% of the time, Pallas kernels for 0%

commit v1 on v0

--- a/solution.py
+++ b/solution.py
@@ -57,7 +57,8 @@
         lax.all_to_all(adj_x, "tile", split_axis=2, concat_axis=1, tiled=True),
     )
     partial_sum = jnp.sum(members.astype(jnp.float32) * row_shaped.astype(jnp.float32), axis=0)
-    group_total = lax.psum(partial_sum, "mem")
+    pieces = lax.all_gather(partial_sum, "mem")
+    group_total = jnp.sum(pieces, axis=0)
     increment = lax.all_to_all(
         group_total.astype(jnp.bfloat16), "tile", split_axis=0, concat_axis=1, tiled=True
     )

time: 567 us -> 515 us (0.908)
  blocking collectives: 197 us -> 0 us
  waiting for transfers between devices: 144 us -> 265 us
  between operations: 1.17 us -> 14.6 us
  local copies, waits for them, and re-layouts: 56.4 us -> 67.5 us
  starting transfers between devices: 42.5 us -> 36.6 us
    psum x1 -> x0, blocking collectives: 197 us -> none  [body(): group_total = lax.psum(partial_sum, 'mem')]
    all_to_all x1, waiting for transfers between devices: 0.01 us -> 75.9 us  [body(): lax.all_to_all(weighted, 'tile', split_axis=1, concat_axis=2, tiled=True)]
    all_gather x0 -> x1, waiting for transfers between devices: none -> 62.2 us  [body(): pieces = lax.all_gather(partial_sum, 'mem')]
    all_to_all x1, waiting for transfers between devices: 57.8 us -> 16.5 us  [body(): lax.all_to_all(adj_x, 'tile', split_axis=2, concat_axis=1, tiled=True)]
    all_to_all x1, waiting for transfers between devices: 9.12 us -> 33.5 us  [body(): lax.all_to_all(group_total.astype(jnp.bfloat16), 'tile', split_axis=0, co...]
    reduce_sum x0 -> x1, local copies, waits for them, and re-layouts: none -> 7.64 us  [body(): jnp.sum(members.astype(jnp.float32) * row_shaped.astype(jnp.float32), axi...]
  transfers between devices with their start and end apart: 6 -> 7, of which waited for: 5 -> 7; matrix products, arithmetic and copies ran while one was open for 19% -> 26% of each run, Pallas kernels for 0% -> 0%
where the time goes in v1:
time: 515 us; the launch traced here: 505 us
  waiting for transfers between devices  265 us (51%)
  other arithmetic  67.9 us (13%)
  local copies, waits for them, and re-layouts  67.5 us (13%)
  matrix products  53.6 us (10%)
  starting transfers between devices  36.6 us (7%)
  between operations  14.6 us (3%)
    all_to_all x1, waiting for transfers between devices, body(): lax.all_to_all(weighted, 'tile', split_axis=1, concat_axis=2, tiled=True)  75.9 us
    all_gather x1, waiting for transfers between devices, body(): pieces = lax.all_gather(partial_sum, 'mem')  62.2 us
    dot_general x2, matrix products, filter_along_x(): jnp.einsum('mzyk,kx->mzyx', fields, filter_x, preferred_element_type=jnp....  36.8 us
    all_to_all x1, waiting for transfers between devices, body(): lax.all_to_all(along, 'tile', split_axis=1, concat_axis=2, tiled=True)  36.2 us
    all_to_all x1, waiting for transfers between devices, body(): lax.all_to_all(group_total.astype(jnp.bfloat16), 'tile', split_axis=0, co...  33.5 us
    all_to_all x1, waiting for transfers between devices, body(): lax.all_to_all(shaped, 'tile', split_axis=2, concat_axis=1, tiled=True)  30.9 us
    convert_element_type x1, other arithmetic, body(): (members.astype(jnp.float32) * grad_rows.astype(jnp.float32)[None]).astyp...  28.4 us
    convert_element_type x2, local copies, waits for them, and re-layouts, filter_along_x(): return jnp.einsum('mzyk,kx->mzyx', fields, filter_x, preferred_element_ty...  19.3 us
  transfers between devices with their start and end apart: 7, of which 7 were waited for; matrix products, arithmetic and copies ran while one was open for 26% of the time, Pallas kernels for 0%

profile of v1, /device:TPU:1, one launch (start us, length us, event | category | flops | bytes accessed | tf_op | source)
XLA Modules:
  0.0 505.3 jit_solution(7507556130286055824)
XLA Ops:
  7.2 1.0 reduce-window.31
  8.1 0.1 slice.18
  8.3 0.1 slice_reduce_fusion
  8.4 0.1 add_bitcast_fusion
  8.4 0.8 copy.49
  9.2 0.1 reduce-window.30
  9.3 0.1 reduce
  9.4 13.6 %fusion.16 = bf16[2,64,12,1536]{3,1,2,0:T(8,128)(2,1)} fusion(f32[1536]{0:T(1024)S(1)} %add_bitcast_fusion, bf16[2,64,12,1536]{3,1,2,0:T(8,128)(2,1)} %param.6, f32[64]{0:T(128)S(1)} %reduce), kind=kOutput, calls=%fused_computation.23 | convolution fusion | flops 7566299136 | bytes 9443584 | tf_op jit(solution)/shard_map/mzyk,kx->mzyx/dot_general | solution.py:32
  23.0 9.7 %copy.51 = bf16[2,64,12,1536]{3,0,2,1:T(2,128)(2,1)} copy(bf16[2,64,12,1536]{3,1,2,0:T(8,128)(2,1)} %fusion.16) | data formatting | bytes 9437184 | tf_op jit(solution)/shard_map/convert_element_type | solution.py:34
  32.7 11.2 %all-to-all-start = ((bf16[2,64,12,1536]{3,0,2,1:T(2,128)(2,1)}), bf16[2,64,12,1536]{3,0,2,1:T(2,128)(2,1)}, u32[]{:S(2)}, u32[]{:S(2)}) async-start(bf16[2,64,12,1536]{3,0,2,1:T(2,128)(2,1)} %copy.51), calls=%async_computation | async-start | bytes 9437184 | tf_op jit(solution)/shard_map/all_to_all | solution.py:50
  43.9 0.0 copy-done
  43.9 5.8 %copy.84 = bf16[1,768,1536]{2,0,1:T(2,128)(2,1)} copy(bf16[1,768,1536]{2,1,0:T(8,128)(2,1)S(1)} %copy-done) | data formatting | bytes 4718592 | tf_op args[2]
  49.8 0.5 broadcast.22
  50.3 15.7 %reduce.7 = bf16[768,1536]{1,0:T(8,128)(2,1)S(1)} reduce(bf16[768,1,1536]{2,1,0:T(2,128)(2,1)} %bitcast.66, bf16[]{:T(256)} %broadcast.22), dimensions={1}, to_apply=%bitcast.65.reduce_sub_computation | reduce | bytes 4718594
  65.9 0.0 copy-start.1
  65.9 2.5 reshape.163
  68.4 36.2 %all-to-all-done = bf16[2,64,12,1536]{3,0,2,1:T(2,128)(2,1)} async-done(((bf16[2,64,12,1536]{3,0,2,1:T(2,128)(2,1)}), bf16[2,64,12,1536]{3,0,2,1:T(2,128)(2,1)}, u32[]{:S(2)}, u32[]{:S(2)}) %all-to-all-start) | async-done | bytes 4718624 | tf_op jit(solution)/shard_map/all_to_all | solution.py:50
  104.6 4.4 all-to-all-start.3
  109.0 0.0 copy-done.1
  109.0 0.3 reduce-window.33
  109.3 0.1 slice.16
  109.4 0.1 slice_reduce_fusion.1
  109.5 0.1 add_bitcast_fusion.1
  109.6 8.4 %convert_bitcast_fusion.2 = bf16[2,1,768,1536]{2,3,0,1:T(8,128)(2,1)} fusion(bf16[2,768,1536]{2,0,1:T(2,128)(2,1)} %bitcast.7, f32[768]{0:T(1024)S(1)} %add_bitcast_fusion.1), kind=kOutput, calls=%fused_computation.21 | convolution fusion | flops 3629187072 | bytes 9440256 | tf_op jit(solution)/shard_map/yk,mzkx->mzyx/dot_general | solution.py:37
  118.0 12.7 %copy.53 = bf16[2,1,768,1536]{3,0,1,2:T(2,128)(2,1)} copy(bf16[2,1,768,1536]{2,3,0,1:T(8,128)(2,1)} %convert_bitcast_fusion.2) | data formatting | bytes 9437184 | tf_op jit(solution)/shard_map/convert_element_type | solution.py:39
  130.7 10.1 %all-to-all-done.3 = bf16[64,2,9216]{2,1,0:T(2,128)(2,1)S(1)} async-done(((bf16[64,2,9216]{2,1,0:T(2,128)(2,1)}), bf16[64,2,9216]{2,1,0:T(2,128)(2,1)S(1)}, u32[]{:S(2)}, u32[]{:S(2)}) %all-to-all-start.3) | async-done | bytes 2359328 | tf_op jit(solution)/shard_map/all_to_all | solution.py:45
  140.7 5.2 %all-to-all-start.1 = ((bf16[2,1,768,1536]{3,0,1,2:T(2,128)(2,1)}), bf16[2,1,768,1536]{3,0,1,2:T(2,128)(2,1)}, u32[]{:S(2)}, u32[]{:S(2)}) async-start(bf16[2,1,768,1536]{3,0,1,2:T(2,128)(2,1)} %copy.53), calls=%async_computation.1 | async-start | bytes 9437184 | tf_op jit(solution)/shard_map/all_to_all | solution.py:56
  146.0 6.7 %reshape.164 = bf16[768,1,1536]{2,1,0:T(2,128)(2,1)} reshape(bf16[64,2,9216]{2,1,0:T(2,128)(2,1)S(1)} %all-to-all-done.3) | data formatting | bytes 4718592
  152.7 16.9 %convert_reduce_fusion = f32[768,1536]{1,0:T(8,128)} fusion(bf16[768,1,1536]{2,1,0:T(2,128)(2,1)} %reshape.164), kind=kLoop, calls=%fused_computation.17 | loop fusion | flops 1179648 | bytes 7077888 | tf_op jit(solution)/shard_map/convert_element_type | solution.py:46
  169.6 6.1 %reshape.152 = f32[64,12,1536]{2,1,0:T(8,128)} reshape(f32[768,1536]{1,0:T(8,128)} %convert_reduce_fusion) | data formatting | bytes 9437184 | tf_op jit(solution)/shard_map/convert_element_type | solution.py:46
  175.7 30.9 %all-to-all-done.1 = bf16[2,1,768,1536]{3,0,1,2:T(2,128)(2,1)} async-done(((bf16[2,1,768,1536]{3,0,1,2:T(2,128)(2,1)}), bf16[2,1,768,1536]{3,0,1,2:T(2,128)(2,1)}, u32[]{:S(2)}, u32[]{:S(2)}) %all-to-all-start.1) | async-done | bytes 4718624 | tf_op jit(solution)/shard_map/all_to_all | solution.py:56
  206.6 28.4 %fusion.1 = (bf16[2,64,12,1536]{3,0,2,1:T(2,128)(2,1)}, f32[64,12,1536]{2,1,0:T(8,128)}) fusion(f32[64,12,1536]{2,1,0:T(8,128)} %reshape.152, bf16[2,64,12,1536]{3,1,2,0:T(8,128)(2,1)} %param.7, bf16[2,64,12,1536]{3,0,2,1:T(2,128)(2,1)} %bitcast.27), kind=kLoop, calls=%fused_computation.3 | loop fusion | flops 12976128 | bytes 23592960 | tf_op jit(solution)/shard_map/convert_element_type | solution.py:46
  235.1 5.3 %all-to-all-start.4 = ((bf16[2,64,12,1536]{3,0,2,1:T(2,128)(2,1)}), bf16[2,64,12,1536]{3,0,2,1:T(2,128)(2,1)}, u32[]{:S(2)}, u32[]{:S(2)}) async-start(bf16[2,64,12,1536]{3,0,2,1:T(2,128)(2,1)} %get-tuple-element.2), calls=%async_computation.4 | async-start | bytes 9437184 | tf_op jit(solution)/shard_map/all_to_all | solution.py:51
  240.3 0.2 all-gather.3.cloned.1.call-start
  240.5 7.6 %copy.54 = f32[64,12,1536]{2,0,1:T(8,128)} copy(f32[64,12,1536]{2,1,0:T(8,128)} %get-tuple-element.3) | data formatting | bytes 9437184 | tf_op jit(solution)/shard_map/reduce_sum | solution.py:59
  248.2 0.0 all-gather.3.cloned.1.call-update
  248.2 75.9 %all-to-all-done.4 = bf16[2,64,12,1536]{3,0,2,1:T(2,128)(2,1)} async-done(((bf16[2,64,12,1536]{3,0,2,1:T(2,128)(2,1)}), bf16[2,64,12,1536]{3,0,2,1:T(2,128)(2,1)}, u32[]{:S(2)}, u32[]{:S(2)}) %all-to-all-start.4) | async-done | bytes 4718624 | tf_op jit(solution)/shard_map/all_to_all | solution.py:51
  324.1 23.2 %convert_bitcast_fusion.1 = bf16[2,1,768,1536]{3,2,0,1:T(8,128)(2,1)} fusion(f32[1536]{0:T(1024)S(1)} %add_bitcast_fusion, bf16[2,768,1536]{2,0,1:T(2,128)(2,1)} %bitcast.15, f32[768]{0:T(1024)S(1)} %add_bitcast_fusion.1), kind=kOutput, calls=%fused_computation.19 | convolution fusion | flops 10891100160 | bytes 9446400 | tf_op jit(solution)/shard_map/mzyk,kx->mzyx/dot_general | solution.py:32
  347.3 9.6 %copy.59 = bf16[2,1,768,1536]{3,0,1,2:T(2,128)(2,1)} copy(bf16[2,1,768,1536]{3,2,0,1:T(8,128)(2,1)} %convert_bitcast_fusion.1) | data formatting | bytes 9437184 | tf_op jit(solution)/shard_map/convert_element_type | solution.py:34
  356.9 5.6 %all-to-all-start.5 = ((bf16[2,1,768,1536]{3,0,1,2:T(2,128)(2,1)}), bf16[2,1,768,1536]{3,0,1,2:T(2,128)(2,1)}, u32[]{:S(2)}, u32[]{:S(2)}) async-start(bf16[2,1,768,1536]{3,0,1,2:T(2,128)(2,1)} %copy.59), calls=%async_computation.5 | async-start | bytes 9437184 | tf_op jit(solution)/shard_map/all_to_all | solution.py:57
  362.5 62.2 %all-gather.3.cloned.1.call-done = f32[128,12,1536]{2,0,1:T(8,128)} async-done(((f32[64,12,1536]{2,0,1:T(8,128)}), f32[128,12,1536]{2,0,1:T(8,128)}) %all-gather.3.cloned.1.call-update) | async-done | bytes 9437200 | tf_op jit(solution)/shard_map/all_gather | solution.py:60
  424.7 5.2 %reduce_sum.19 = bf16[64,12,1536]{2,0,1:T(8,128)(2,1)S(1)} reduce(f32[2,64,12,1536]{3,1,0,2:T(8,128)} %bitcast.67, f32[]{:T(128)} %constant.9.clone.1), dimensions={0}, to_apply=%region_6.7 | reduce | flops 1179648 | bytes 11796484 | tf_op jit(solution)/shard_map/reduce_sum | solution.py:61
  429.9 3.0 copy.55
  432.9 16.5 %all-to-all-done.5 = bf16[2,1,768,1536]{3,0,1,2:T(2,128)(2,1)} async-done(((bf16[2,1,768,1536]{3,0,1,2:T(2,128)(2,1)}), bf16[2,1,768,1536]{3,0,1,2:T(2,128)(2,1)}, u32[]{:S(2)}, u32[]{:S(2)}) %all-to-all-start.5) | async-done | bytes 4718624 | tf_op jit(solution)/shard_map/all_to_all | solution.py:57
  449.4 4.7 all-to-all-start.2
  454.1 8.3 %convert_bitcast_fusion = bf16[2,64,12,1536]{3,1,2,0:T(8,128)(2,1)} fusion(bf16[2,64,12,1536]{3,0,2,1:T(2,128)(2,1)} %bitcast.21, f32[64]{0:T(128)S(1)} %reduce), kind=kOutput, calls=%fused_computation.18 | convolution fusion | flops 304386048 | bytes 9437440 | tf_op jit(solution)/shard_map/wz,mwyx->mzyx/dot_general | solution.py:65
  462.4 33.5 %all-to-all-done.2 = bf16[64,12,1536]{2,1,0:T(8,128)(2,1)S(1)} async-done(((bf16[64,12,1536]{2,1,0:T(8,128)(2,1)}), bf16[64,12,1536]{2,1,0:T(8,128)(2,1)S(1)}, u32[]{:S(2)}, u32[]{:S(2)}) %all-to-all-start.2) | async-done | bytes 2359328 | tf_op jit(solution)/shard_map/all_to_all | solution.py:62
  495.9 2.1 all_to_all.19
  (3 shorter events, 0.1 us)
Async XLA Ops:
  32.7 11.2 %copy-start = (bf16[1,768,1536]{2,1,0:T(8,128)(2,1)S(1)}, bf16[1,768,1536]{2,1,0:T(8,128)(2,1)}, u32[]{:S(2)}) copy-start(bf16[1,768,1536]{2,1,0:T(8,128)(2,1)} %param.8) | copy-start | bytes 7077892
  32.7 71.9 %all-to-all-start = ((bf16[2,64,12,1536]{3,0,2,1:T(2,128)(2,1)}), bf16[2,64,12,1536]{3,0,2,1:T(2,128)(2,1)}, u32[]{:S(2)}, u32[]{:S(2)}) async-start(bf16[2,64,12,1536]{3,0,2,1:T(2,128)(2,1)} %copy.51), calls=%async_computation | async-start | bytes 9437184 | tf_op jit(solution)/shard_map/all_to_all | solution.py:50
  65.9 43.1 %copy-start.1 = (f32[768]{0:T(1024)S(1)}, f32[768]{0:T(1024)}, u32[]{:S(2)}) copy-start(f32[768]{0:T(1024)} %param.10) | copy-start | bytes 9220
  104.6 36.1 %all-to-all-start.3 = ((bf16[64,2,9216]{2,1,0:T(2,128)(2,1)}), bf16[64,2,9216]{2,1,0:T(2,128)(2,1)S(1)}, u32[]{:S(2)}, u32[]{:S(2)}) async-start(bf16[64,2,9216]{2,1,0:T(2,128)(2,1)} %reshape.163), calls=%async_computation.3 | async-start | bytes 4718592 | tf_op jit(solution)/shard_map/all_to_all | solution.py:45
  140.7 65.9 %all-to-all-start.1 = ((bf16[2,1,768,1536]{3,0,1,2:T(2,128)(2,1)}), bf16[2,1,768,1536]{3,0,1,2:T(2,128)(2,1)}, u32[]{:S(2)}, u32[]{:S(2)}) async-start(bf16[2,1,768,1536]{3,0,1,2:T(2,128)(2,1)} %copy.53), calls=%async_computation.1 | async-start | bytes 9437184 | tf_op jit(solution)/shard_map/all_to_all | solution.py:56
  235.1 89.0 %all-to-all-start.4 = ((bf16[2,64,12,1536]{3,0,2,1:T(2,128)(2,1)}), bf16[2,64,12,1536]{3,0,2,1:T(2,128)(2,1)}, u32[]{:S(2)}, u32[]{:S(2)}) async-start(bf16[2,64,12,1536]{3,0,2,1:T(2,128)(2,1)} %get-tuple-element.2), calls=%async_computation.4 | async-start | bytes 9437184 | tf_op jit(solution)/shard_map/all_to_all | solution.py:51
  240.3 184.4 %all-gather.3.cloned.1.call-start = ((), (), s32[]{:S(2)}) async-start(), calls=%async_computation.6 | async-start | bytes 14155776 | tf_op jit(solution)/shard_map/all_gather | solution.py:60
  356.9 92.5 %all-to-all-start.5 = ((bf16[2,1,768,1536]{3,0,1,2:T(2,128)(2,1)}), bf16[2,1,768,1536]{3,0,1,2:T(2,128)(2,1)}, u32[]{:S(2)}, u32[]{:S(2)}) async-start(bf16[2,1,768,1536]{3,0,1,2:T(2,128)(2,1)} %copy.59), calls=%async_computation.5 | async-start | bytes 9437184 | tf_op jit(solution)/shard_map/all_to_all | solution.py:57
  449.4 46.5 %all-to-all-start.2 = ((bf16[64,12,1536]{2,1,0:T(8,128)(2,1)}), bf16[64,12,1536]{2,1,0:T(8,128)(2,1)S(1)}, u32[]{:S(2)}, u32[]{:S(2)}) async-start(bf16[64,12,1536]{2,1,0:T(8,128)(2,1)} %copy.55), calls=%async_computation.2 | async-start | bytes 6291456 | tf_op jit(solution)/shard_map/all_to_all | solution.py:62
Sparse Core Ops, SparseCore 0:
  248.3 176.3 all-gather.2
